TPU v7x, 256 devices: a whole 4x4x8 slice. The times are simulated.
256 devices in a mesh: pts: 128 (over y, x, z_lo, core), grp: 2 (over z_hi).
Axes of the slice: x: 4, y: 4, z: 8 (z_hi: 2, z_lo: 4; z = z_hi * 4 + z_lo), core: 2. Of those that a mesh axis runs over, the one named last changes fastest.
Arguments:
- grid_states: float32 [59, 2097152], P(None, ('pts', 'grp')), may hold values from 0 to 1
- coarse_active: int32 [16384, 8], P(('pts', 'grp')), may hold values from 0 to 127, all different within a row
- fine_active: int32 [16384, 8], P(('pts', 'grp')), may hold values from 0 to 31, all different within a row
- shock: int32 [2097152], P(('pts', 'grp')), may hold values from 0 to 3
- coarse_surplus: bfloat16 [4, 60, 16384], P(None, 'grp', 'pts'), may hold values from -0.796875 to 0.796875
- fine_surplus: bfloat16 [4, 60, 524288], P(None, 'grp', 'pts'), may hold values from -0.796875 to 0.796875
- coarse_dim: int32 [128], P('pts'), may hold values from 0 to 58
- coarse_level: int32 [128], P('pts'), may hold values from 0 to 2
- fine_dim: int32 [4096], P('pts'), may hold values from 0 to 58
- fine_level: int32 [4096], P('pts'), may hold values from 0 to 2
- tfp: float32 [4], replicated, may hold values from 0.5 to 2
- trans_weight: float32 [4, 4], replicated, may hold values from 0.2 to 5
Outputs:
- savings: bfloat16 [4, 60, 2097152], P(None, None, ('pts', 'grp'))
- prices: float32 [2, 2097152], P(None, ('pts', 'grp'))
Inputs may be any that keep to these rules, and one draw needn't show every extreme that they name: `coarse_active`: each row names 8 different coarse blocks, and every coarse block is named by some row. `fine_active`: each row names 8 different fine blocks of its region.
All inputs are finite; a program needn't handle non-finite values.
Results may differ from a plain program's by a relative error of at most 0.0034.
Values may be sent and summed in bfloat16 or wider, within the bound.
A program may use at most 128 MiB of HBM per device.

v0:
```python
import math

import jax
import jax.numpy as jnp
from jax import lax
from jax.sharding import PartitionSpec as P

S = 4
GEN = 60
BS = 128


def evaluate(states, active, table, dims_all, levels_all):
    nstate, npoints = states.shape
    tiles, nactive = active.shape
    tile = npoints // tiles
    block_size = table.shape[2]
    turns = math.gcd(tiles, 8)
    group = tiles // turns
    grouped = states.reshape(nstate, turns, group, tile).transpose(1, 2, 0, 3)
    active_grouped = active.reshape(turns, group, nactive)
    offsets = jnp.arange(block_size, dtype=jnp.float32)

    def one_tile(states_tile, block_ids):
        scales = (block_size - 1) * jnp.exp2(-levels_all[block_ids].astype(jnp.float32))
        scaled = scales[:, None] * states_tile[dims_all[block_ids]]
        phi = jnp.maximum(0.0, 1.0 - jnp.abs(scaled[:, None, :] - offsets[None, :, None])).astype(
            jnp.bfloat16
        )
        coef = table[block_ids]
        return jnp.einsum("kgj,kjt->gt", coef, phi, preferred_element_type=jnp.float32)

    def one_turn(pair):
        return jax.vmap(one_tile)(pair[0], pair[1])

    values = lax.map(one_turn, (grouped, active_grouped))
    return values.transpose(2, 0, 1, 3).reshape(table.shape[1], npoints)


def to_table(gathered):
    shocks, gens, basis = gathered.shape
    nblocks = basis // BS
    return gathered.reshape(shocks * gens, nblocks, BS).transpose(1, 0, 2)


def joined(coarse_all, fine_local, coarse_ids, fine_ids):
    table = jnp.concatenate([to_table(coarse_all), to_table(fine_local)], axis=0)
    ncoarse = coarse_all.shape[2] // BS
    ids = jnp.concatenate([coarse_ids, fine_ids + ncoarse], axis=1)
    return (table, ids)


def expected_prices(savings, shock, tfp, trans_weight):
    capital = jnp.mean(savings.astype(jnp.float32), axis=1)
    interest = 0.33 * tfp[:, None] * capital ** (0.33 - 1.0) + 1.0 - 0.1
    earnings = (1.0 - 0.33) * tfp[:, None] * capital**0.33
    transition = trans_weight / jnp.sum(trans_weight, axis=1, keepdims=True)
    onehot = (shock[None, :] == jnp.arange(S, dtype=jnp.int32)[:, None]).astype(jnp.float32)
    weights = jnp.dot(transition.T, onehot, precision=lax.Precision.HIGHEST)
    return jnp.stack([jnp.sum(weights * interest, axis=0), jnp.sum(weights * earnings, axis=0)])


def body(
    grid_states,
    coarse_active,
    fine_active,
    shock,
    coarse_surplus,
    fine_surplus,
    coarse_dim,
    coarse_level,
    fine_dim,
    fine_level,
    tfp,
    trans_weight,
):
    npoints = grid_states.shape[1]
    coarse_gens, fine_gens = (
        lax.all_gather(coarse_surplus, "grp", axis=1, tiled=True),
        lax.all_gather(fine_surplus, "grp", axis=1, tiled=True),
    )
    coarse_all, dims_coarse, levels_coarse = (
        lax.all_gather(coarse_gens, "pts", axis=2, tiled=True),
        lax.all_gather(coarse_dim, "pts", axis=0, tiled=True),
        lax.all_gather(coarse_level, "pts", axis=0, tiled=True),
    )
    table, block_ids = joined(coarse_all, fine_gens, coarse_active, fine_active)
    dims_all = jnp.concatenate([dims_coarse, fine_dim])
    levels_all = jnp.concatenate([levels_coarse, fine_level])
    log_savings = evaluate(grid_states, block_ids, table, dims_all, levels_all)
    savings = jnp.exp(log_savings).astype(jnp.bfloat16).reshape(S, GEN, npoints)
    prices = expected_prices(savings, shock, tfp, trans_weight)
    return (savings, prices)


def solution(mesh):
    in_specs = (
        P(None, ("pts", "grp")),
        P(("pts", "grp"), None),
        P(("pts", "grp"), None),
        P(("pts", "grp")),
        P(None, "grp", "pts"),
        P(None, "grp", "pts"),
        P("pts"),
        P("pts"),
        P("pts"),
        P("pts"),
        P(),
        P(),
    )
    out_specs = (P(None, None, ("pts", "grp")), P(None, ("pts", "grp")))
    return jax.shard_map(body, mesh=mesh, in_specs=in_specs, out_specs=out_specs, check_vma=False)
```

profile of v0, /device:TPU:36, one launch (start us, length us, event | category | flops | bytes accessed | tf_op | source)
XLA Modules:
  0.0 536.3 jit_solution(2822092789721412001)
XLA Ops:
  7.9 10.8 %all_gather.15 = bf16[4,60,128]{2,0,1:T(4,128)(2,1)} all-gather(bf16[4,30,128]{2,0,1:T(4,128)(2,1)} %param.18), channel_id=1, replica_groups=mesh['pts'=128,'grp'=2] {'grp'}, dimensions={1}, use_global_device_ids=true | all-gather | bytes 92160 | tf_op jit(solution)/shard_map/all_gather | solution.py:79
  20.1 2.0 copy.31
  23.5 1.3 dynamic-slice
  27.1 20.8 %all-reduce.2 = (s32[128]{0:T(128)S(1)}, s32[128]{0:T(128)S(1)}) all-reduce(s32[128]{0:T(128)S(1)} %dynamic-update-slice, s32[128]{0:T(128)S(1)} %dynamic-update-slice.1), channel_id=1, replica_groups=mesh['pts'=128,'grp'=2] {'pts'}, use_global_device_ids=true, to_apply=%add | all-reduce | flops 256 | bytes 2048
  49.3 1.5 bitcast_bitcast_fusion
  50.8 22.7 %all-gather.5.cloned.1.call-done = bf16[4,60,4096]{2,0,1:T(4,128)(2,1)} async-done(((bf16[4,30,4096]{2,0,1:T(4,128)(2,1)}), bf16[4,60,4096]{2,0,1:T(4,128)(2,1)}) %all-gather.5.cloned.1.call-update) | async-done | bytes 1966096 | tf_op jit(solution)/shard_map/all_gather | solution.py:80
  73.5 2.6 copy.24
  76.2 2.0 reshape.81
  78.2 212.4 %all-gather.3.cloned.1.call-done = bf16[4,60,16384]{2,0,1:T(4,128)(2,1)} async-done(((bf16[4,60,128]{2,0,1:T(4,128)(2,1)}), bf16[4,60,16384]{2,0,1:T(4,128)(2,1)}) %all-gather.3.cloned.1.call-update) | async-done | bytes 7864336 | tf_op jit(solution)/shard_map/all_gather | solution.py:83
  290.6 10.9 %copy.23 = bf16[4,60,16384]{2,1,0:T(8,128)(2,1)} copy(bf16[4,60,16384]{2,0,1:T(4,128)(2,1)} %all-gather.3.cloned.1.call-done) | data formatting | bytes 15728640 | tf_op jit(solution)/shard_map/all_gather | solution.py:83
  301.5 9.1 %reshape.80 = bf16[240,128,128]{2,1,0:T(8,128)(2,1)} reshape(bf16[4,60,16384]{2,1,0:T(8,128)(2,1)} %copy.23) | data formatting | bytes 15728640 | tf_op jit(solution)/shard_map/reshape | solution.py:43
  310.6 8.5 %pad_maximum_fusion = bf16[160,240,128]{2,0,1:T(8,128)(2,1)} fusion(bf16[32,240,128]{2,0,1:T(8,128)(2,1)S(1)} %bitcast.50, bf16[128,240,128]{2,0,1:T(8,128)(2,1)} %bitcast.49), kind=kLoop, calls=%fused_computation.27 | loop fusion | flops 19660800 | bytes 19660800 | tf_op jit(solution)/shard_map/concatenate | solution.py:47
  319.1 11.3 %copy.25 = bf16[160,240,128]{2,1,0:T(8,128)(2,1)} copy(bf16[160,240,128]{2,0,1:T(8,128)(2,1)} %pad_maximum_fusion) | data formatting | bytes 19660800
  330.4 174.7 %while.11 = (s32[]{:T(128)}, f32[8,8,240,128]{3,2,1,0:T(8,128)}, s32[8,8,16]{2,1,0:T(8,128)S(1)}, bf16[160,240,128]{2,1,0:T(8,128)(2,1)}, s32[160]{0:T(256)S(1)}...) while((s32[]{:T(128)}, f32[8,8,240,128]{3,2,1,0:T(8,128)}, ...), condition=%wide.region_1.2_spmd.clone, body=%wide.region_0.1_spmd.clone.sunk | while | flops 1017138048 | bytes 25404508 | solution.py:36
  330.5 1.3 gather_fusion.1
  333.9 1.3 gather_fusion.3
  335.4 10.4 %gather_fusion = bf16[128,240,128]{2,1,0:T(8,128)(2,1)} fusion(bf16[160,240,128]{2,1,0:T(8,128)(2,1)} %get-tuple-element.163, s32[1024]{0:T(1024)S(1)} %pad_clamp_fusion.2), kind=kCustom, calls=%fused_computation.clone.clone.1 | custom fusion | bytes 15729152 | tf_op jit(solution)/shard_map/while/body/eval_jaxpr/vmap()/gather | solution.py:30
  345.8 6.5 %fusion.35 = f32[8,8,240,128]{3,2,1,0:T(8,128)} fusion(f32[8,8,240,128]{3,2,1,0:T(8,128)} %get-tuple-element.153, s32[]{:T(128)} %get-tuple-element.152, bf16[8,16,240,128]{3,2,1,0:T(8,128)(2,1)} %bitcast.48, f32[8,16,128]{2,1,0:T(8,128)S(1)} %broadcast_multiply_fusion.4), kind=kOutput, calls=%fused_computation.15.clone.1 | convolution fusion | flops 1017118720 | bytes 8913408 | tf_op jit(solution)/shard_map/while/body/eval_jaxpr/vmap(kgj,kjt->gt)/dot_general | solution.py:31
  352.4 1.3 gather_fusion.1
  355.7 1.3 gather_fusion.3
  357.2 10.4 %gather_fusion = bf16[128,240,128]{2,1,0:T(8,128)(2,1)} fusion(bf16[160,240,128]{2,1,0:T(8,128)(2,1)} %get-tuple-element.163, s32[1024]{0:T(1024)S(1)} %pad_clamp_fusion.2), kind=kCustom, calls=%fused_computation.clone.clone.1 | custom fusion | bytes 15729152 | tf_op jit(solution)/shard_map/while/body/eval_jaxpr/vmap()/gather | solution.py:30
  367.6 6.5 %fusion.35 = f32[8,8,240,128]{3,2,1,0:T(8,128)} fusion(f32[8,8,240,128]{3,2,1,0:T(8,128)} %get-tuple-element.153, s32[]{:T(128)} %get-tuple-element.152, bf16[8,16,240,128]{3,2,1,0:T(8,128)(2,1)} %bitcast.48, f32[8,16,128]{2,1,0:T(8,128)S(1)} %broadcast_multiply_fusion.4), kind=kOutput, calls=%fused_computation.15.clone.1 | convolution fusion | flops 1017118720 | bytes 8913408 | tf_op jit(solution)/shard_map/while/body/eval_jaxpr/vmap(kgj,kjt->gt)/dot_general | solution.py:31
  374.2 1.3 gather_fusion.1
  377.6 1.3 gather_fusion.3
  379.0 10.4 %gather_fusion = bf16[128,240,128]{2,1,0:T(8,128)(2,1)} fusion(bf16[160,240,128]{2,1,0:T(8,128)(2,1)} %get-tuple-element.163, s32[1024]{0:T(1024)S(1)} %pad_clamp_fusion.2), kind=kCustom, calls=%fused_computation.clone.clone.1 | custom fusion | bytes 15729152 | tf_op jit(solution)/shard_map/while/body/eval_jaxpr/vmap()/gather | solution.py:30
  389.5 6.5 %fusion.35 = f32[8,8,240,128]{3,2,1,0:T(8,128)} fusion(f32[8,8,240,128]{3,2,1,0:T(8,128)} %get-tuple-element.153, s32[]{:T(128)} %get-tuple-element.152, bf16[8,16,240,128]{3,2,1,0:T(8,128)(2,1)} %bitcast.48, f32[8,16,128]{2,1,0:T(8,128)S(1)} %broadcast_multiply_fusion.4), kind=kOutput, calls=%fused_computation.15.clone.1 | convolution fusion | flops 1017118720 | bytes 8913408 | tf_op jit(solution)/shard_map/while/body/eval_jaxpr/vmap(kgj,kjt->gt)/dot_general | solution.py:31
  396.0 1.3 gather_fusion.1
  399.4 1.3 gather_fusion.3
  400.9 10.4 %gather_fusion = bf16[128,240,128]{2,1,0:T(8,128)(2,1)} fusion(bf16[160,240,128]{2,1,0:T(8,128)(2,1)} %get-tuple-element.163, s32[1024]{0:T(1024)S(1)} %pad_clamp_fusion.2), kind=kCustom, calls=%fused_computation.clone.clone.1 | custom fusion | bytes 15729152 | tf_op jit(solution)/shard_map/while/body/eval_jaxpr/vmap()/gather | solution.py:30
  411.3 6.4 %fusion.35 = f32[8,8,240,128]{3,2,1,0:T(8,128)} fusion(f32[8,8,240,128]{3,2,1,0:T(8,128)} %get-tuple-element.153, s32[]{:T(128)} %get-tuple-element.152, bf16[8,16,240,128]{3,2,1,0:T(8,128)(2,1)} %bitcast.48, f32[8,16,128]{2,1,0:T(8,128)S(1)} %broadcast_multiply_fusion.4), kind=kOutput, calls=%fused_computation.15.clone.1 | convolution fusion | flops 1017118720 | bytes 8913408 | tf_op jit(solution)/shard_map/while/body/eval_jaxpr/vmap(kgj,kjt->gt)/dot_general | solution.py:31
  417.9 1.3 gather_fusion.1
  422.7 10.4 %gather_fusion = bf16[128,240,128]{2,1,0:T(8,128)(2,1)} fusion(bf16[160,240,128]{2,1,0:T(8,128)(2,1)} %get-tuple-element.163, s32[1024]{0:T(1024)S(1)} %pad_clamp_fusion.2), kind=kCustom, calls=%fused_computation.clone.clone.1 | custom fusion | bytes 15729152 | tf_op jit(solution)/shard_map/while/body/eval_jaxpr/vmap()/gather | solution.py:30
  433.1 6.5 %fusion.35 = f32[8,8,240,128]{3,2,1,0:T(8,128)} fusion(f32[8,8,240,128]{3,2,1,0:T(8,128)} %get-tuple-element.153, s32[]{:T(128)} %get-tuple-element.152, bf16[8,16,240,128]{3,2,1,0:T(8,128)(2,1)} %bitcast.48, f32[8,16,128]{2,1,0:T(8,128)S(1)} %broadcast_multiply_fusion.4), kind=kOutput, calls=%fused_computation.15.clone.1 | convolution fusion | flops 1017118720 | bytes 8913408 | tf_op jit(solution)/shard_map/while/body/eval_jaxpr/vmap(kgj,kjt->gt)/dot_general | solution.py:31
  439.7 1.3 gather_fusion.1
  443.1 1.3 gather_fusion.3
  444.5 10.4 %gather_fusion = bf16[128,240,128]{2,1,0:T(8,128)(2,1)} fusion(bf16[160,240,128]{2,1,0:T(8,128)(2,1)} %get-tuple-element.163, s32[1024]{0:T(1024)S(1)} %pad_clamp_fusion.2), kind=kCustom, calls=%fused_computation.clone.clone.1 | custom fusion | bytes 15729152 | tf_op jit(solution)/shard_map/while/body/eval_jaxpr/vmap()/gather | solution.py:30
  455.0 6.5 %fusion.35 = f32[8,8,240,128]{3,2,1,0:T(8,128)} fusion(f32[8,8,240,128]{3,2,1,0:T(8,128)} %get-tuple-element.153, s32[]{:T(128)} %get-tuple-element.152, bf16[8,16,240,128]{3,2,1,0:T(8,128)(2,1)} %bitcast.48, f32[8,16,128]{2,1,0:T(8,128)S(1)} %broadcast_multiply_fusion.4), kind=kOutput, calls=%fused_computation.15.clone.1 | convolution fusion | flops 1017118720 | bytes 8913408 | tf_op jit(solution)/shard_map/while/body/eval_jaxpr/vmap(kgj,kjt->gt)/dot_general | solution.py:31
  461.5 1.3 gather_fusion.1
  466.4 10.4 %gather_fusion = bf16[128,240,128]{2,1,0:T(8,128)(2,1)} fusion(bf16[160,240,128]{2,1,0:T(8,128)(2,1)} %get-tuple-element.163, s32[1024]{0:T(1024)S(1)} %pad_clamp_fusion.2), kind=kCustom, calls=%fused_computation.clone.clone.1 | custom fusion | bytes 15729152 | tf_op jit(solution)/shard_map/while/body/eval_jaxpr/vmap()/gather | solution.py:30
  476.8 6.5 %fusion.35 = f32[8,8,240,128]{3,2,1,0:T(8,128)} fusion(f32[8,8,240,128]{3,2,1,0:T(8,128)} %get-tuple-element.153, s32[]{:T(128)} %get-tuple-element.152, bf16[8,16,240,128]{3,2,1,0:T(8,128)(2,1)} %bitcast.48, f32[8,16,128]{2,1,0:T(8,128)S(1)} %broadcast_multiply_fusion.4), kind=kOutput, calls=%fused_computation.15.clone.1 | convolution fusion | flops 1017118720 | bytes 8913408 | tf_op jit(solution)/shard_map/while/body/eval_jaxpr/vmap(kgj,kjt->gt)/dot_general | solution.py:31
  483.4 1.3 gather_fusion.1
  488.2 10.4 %gather_fusion = bf16[128,240,128]{2,1,0:T(8,128)(2,1)} fusion(bf16[160,240,128]{2,1,0:T(8,128)(2,1)} %get-tuple-element.163, s32[1024]{0:T(1024)S(1)} %pad_clamp_fusion.2), kind=kCustom, calls=%fused_computation.clone.clone.1 | custom fusion | bytes 15729152 | tf_op jit(solution)/shard_map/while/body/eval_jaxpr/vmap()/gather | solution.py:30
  498.6 6.4 %fusion.35 = f32[8,8,240,128]{3,2,1,0:T(8,128)} fusion(f32[8,8,240,128]{3,2,1,0:T(8,128)} %get-tuple-element.153, s32[]{:T(128)} %get-tuple-element.152, bf16[8,16,240,128]{3,2,1,0:T(8,128)(2,1)} %bitcast.48, f32[8,16,128]{2,1,0:T(8,128)S(1)} %broadcast_multiply_fusion.4), kind=kOutput, calls=%fused_computation.15.clone.1 | convolution fusion | flops 1017118720 | bytes 8913408 | tf_op jit(solution)/shard_map/while/body/eval_jaxpr/vmap(kgj,kjt->gt)/dot_general | solution.py:31
  505.1 4.3 fusion.22
  509.4 2.9 copy.27
  512.3 5.5 %convert_element_type.26 = bf16[4,60,8192]{2,1,0:T(8,128)(2,1)} reshape(bf16[240,8,8,128]{3,2,1,0:T(8,128)(2,1)} %copy.27) | data formatting | bytes 7864320 | tf_op jit(solution)/shard_map/convert_element_type | solution.py:91
  517.8 3.0 convert_reduce_fusion
  520.9 7.1 %copy.28 = bf16[4,60,8192]{2,0,1:T(4,128)(2,1)} copy(bf16[4,60,8192]{2,1,0:T(8,128)(2,1)} %convert_element_type.26) | data formatting | bytes 7864320
  (114 shorter events, 30.0 us)
Async XLA Ops:
  7.2 66.4 %all-gather.5.cloned.1.call-start = ((), (), s32[]{:S(2)}) async-start(), calls=%async_computation.1 | async-start | bytes 2949120 | tf_op jit(solution)/shard_map/all_gather | solution.py:80
  7.9 282.7 %all-gather.3.cloned.1.call-start = ((), (), s32[]{:S(2)}) async-start(), calls=%async_computation | async-start | bytes 7925760 | tf_op jit(solution)/shard_map/all_gather | solution.py:83
  301.5 9.1 %copy-start = (bf16[240,32,128]{2,1,0:T(8,128)(2,1)S(1)}, bf16[240,32,128]{2,1,0:T(8,128)(2,1)}, u32[]{:S(2)}) copy-start(bf16[240,32,128]{2,1,0:T(8,128)(2,1)} %reshape.81) | copy-start | bytes 5898244
  517.8 10.2 %copy-start.1 = (f32[4,4]{1,0:T(4,128)S(1)}, f32[4,4]{1,0:T(4,128)}, u32[]{:S(2)}) copy-start(f32[4,4]{1,0:T(4,128)} %param.25) | copy-start | bytes 196
  517.8 10.2 %copy-start.2 = (s32[8192]{0:T(1024)S(1)}, s32[8192]{0:T(1024)}, u32[]{:S(2)}) copy-start(s32[8192]{0:T(1024)} %param.17) | copy-start | bytes 98308
Sparse Core Ops, SparseCore 0:
  9.8 63.7 all-gather.4
  75.3 215.2 all-gather.2
where the time goes:
time: 542 us; the launch traced here: 536 us
  waiting for transfers between devices  236 us (44%)
  local copies, waits for them, and re-layouts  180 us (33%)
  matrix products  52.4 us (10%)
  blocking collectives  31.7 us (6%)
  other arithmetic  20.9 us (4%)
  between operations  15.4 us (3%)
    all_gather x1, waiting for transfers between devices, body(): lax.all_gather(coarse_gens, 'pts', axis=2, tiled=True)  212 us
    gather x8, local copies, waits for them, and re-layouts, one_tile(): coef = table[block_ids]  83.5 us
    dot_general x8, matrix products, one_tile(): jnp.einsum('kgj,kjt->gt', coef, phi, preferred_element_type=jnp.float32)  51.7 us
    unnamed x14, local copies, waits for them, and re-layouts  23.3 us
    all_gather x1, waiting for transfers between devices, body(): lax.all_gather(fine_surplus, 'grp', axis=1, tiled=True)  22.7 us
    unnamed x1, blocking collectives  20.8 us
    gather x32, local copies, waits for them, and re-layouts, one_tile(): scaled = scales[:, None] * states_tile[dims_all[block_ids]]  19.1 us
    reshape x2, local copies, waits for them, and re-layouts, to_table(): return gathered.reshape(shocks * gens, nblocks, BS).transpose(1, 0, 2)  11.1 us
  transfers between devices with their start and end apart: 2, of which 2 were waited for; matrix products, arithmetic and copies ran while one was open for 3% of the time, Pallas kernels for 0%

commit v1 on v0

v1 whole, which is shorter than its diff:
```python
import functools

import jax
import jax.numpy as jnp
from jax import lax
from jax.experimental import pallas as pl
from jax.experimental.pallas import tpu as pltpu
from jax.sharding import PartitionSpec as P

MESH = pl.DeviceIdType.MESH


def gather_kernel(piece, fine, G, F, zs, zr, xs, xr, ys, yr, ss, sr, fs, fr, ls):
    p, g = lax.axis_index("pts"), lax.axis_index("grp")
    c, zl, x, y = p % 2, (p // 2) % 4, (p // 8) % 4, p // 32
    z = g * 4 + zl
    def dev(x, y, z, c):
        return {"pts": ((y * 4 + x) * 4 + z % 4) * 2 + c, "grp": z // 4}
    zd = lambda d: dev(x, y, (z + d + 8) % 8, c)
    xd = lambda d: dev((x + d + 4) % 4, y, z, c)
    yd = lambda d: dev(x, (y + d + 4) % 4, z, c)
    sib = dev(x, y, z, 1 - c)
    zo, xo = (4, 3, -3, 2, -2, 1, -1), (2, 1, -1)
    b = pltpu.get_barrier_semaphore()
    partners = [zd(d) for d in zo] + [xd(d) for d in xo] + [yd(d) for d in xo] + [sib]
    for d in partners:
        pl.semaphore_signal(b, 1, device_id=d, device_id_type=MESH)
    pl.semaphore_wait(b, len(partners))
    pend = []
    def rc(src, dst, s, r, d):
        cp = pltpu.make_async_remote_copy(src, dst, s, r, device_id=d, device_id_type=MESH)
        cp.start()
        pend.append(cp)
        return cp
    own = pltpu.make_async_copy(piece, G.at[c, z, y, x], ls)
    zc = [rc(piece, G.at[c, z, y, x], zs.at[i], zr.at[i], zd(d)) for i, d in enumerate(zo)]
    own.start()
    rc(fine, F, fs, fr, zd(4))
    own.wait()
    for cp in zc: cp.wait_recv()
    a = G.at[c, pl.ds(0, 4), y, x]
    bb = G.at[c, pl.ds(4, 4), y, x]
    s1 = []
    for i, d in enumerate(xo):
        s1.append(rc(a, a, xs.at[i], xr.at[i], xd(d)))
        s1.append(rc(bb, bb, ys.at[i], yr.at[i], yd(d)))
    for cp in s1: cp.wait_recv()
    def A(yy, z0=0, nz=4): return G.at[c, pl.ds(z0, nz), yy]
    def B(xx, z0=4, nz=4): return G.at[c, pl.ds(z0, nz), :, xx]
    def sibs(i, ref): rc(ref, ref, ss.at[i], sr.at[i], sib)
    ym, yp, xm, xp = (y + 3) % 4, (y + 1) % 4, (x + 3) % 4, (x + 1) % 4
    y2, x2 = (y + 2) % 4, (x + 2) % 4
    u = [rc(A(y), A(y), ys.at[3], yr.at[3], yd(1)), rc(B(x), B(x), xs.at[3], xr.at[3], xd(1)),
         rc(A(y), A(y), ys.at[4], yr.at[4], yd(-1)), rc(B(x), B(x), xs.at[4], xr.at[4], xd(-1))]
    sibs(0, A(y)); sibs(1, B(x))
    v = []
    u[0].wait_recv(); v.append(rc(A(ym, 0, 2), A(ym, 0, 2), ys.at[5], yr.at[5], yd(1))); sibs(2, A(ym))
    u[1].wait_recv(); v.append(rc(B(xm, 4, 2), B(xm, 4, 2), xs.at[5], xr.at[5], xd(1))); sibs(3, B(xm))
    u[2].wait_recv(); v.append(rc(A(yp, 2, 2), A(yp, 2, 2), ys.at[6], yr.at[6], yd(-1))); sibs(4, A(yp))
    u[3].wait_recv(); v.append(rc(B(xp, 6, 2), B(xp, 6, 2), xs.at[6], xr.at[6], xd(-1))); sibs(5, B(xp))
    for cp in v: cp.wait_recv()
    sibs(6, A(y2)); sibs(7, B(x2))
    done = set(id(q) for q in zc + s1 + u + v)
    for cp in pend:
        cp.wait_send()
        if id(cp) not in done: cp.wait_recv()

def gather(piece, fine):
    dma = pltpu.SemaphoreType.DMA
    return pl.pallas_call(gather_kernel,
        out_shape=(jax.ShapeDtypeStruct((2,8,4,4,128,128), jnp.bfloat16), jax.ShapeDtypeStruct((30,4,4096), jnp.bfloat16)),
        in_specs=[pl.BlockSpec(memory_space=pl.ANY)]*2, out_specs=[pl.BlockSpec(memory_space=pl.ANY)]*2,
        scratch_shapes=[dma((7,)), dma((7,)), dma((7,)), dma((7,)), dma((7,)), dma((7,)), dma((8,)), dma((8,)), dma, dma, dma],
        compiler_params=pltpu.CompilerParams(collective_id=0, has_side_effects=True))(piece, fine)


TPS = 8

def hat_rows(states, lane0, dim, level, low_ref):
    row = jnp.broadcast_to(states[pl.ds(lane0 * 64 + dim, 1), :], (16, 128))
    scale = jnp.where(level == 0, 127.0, jnp.where(level == 1, 63.5, 31.75))
    scaled = row * scale
    lower = jnp.clip(jnp.floor(scaled), 0.0, 126.0)
    lo = jnp.maximum(0.0, 1.0 - jnp.abs(scaled - lower)).astype(jnp.bfloat16)
    hi = jnp.maximum(0.0, 1.0 - jnp.abs(scaled - lower - 1.0)).astype(jnp.bfloat16)
    at = lower.astype(jnp.bfloat16)
    out = []
    zero = jnp.zeros((16, 128), jnp.bfloat16)
    for q in range(8):
        j = low_ref[pl.ds(16 * q, 16), :]
        t = j - at
        out.append(jnp.where(t == 0, lo, jnp.where(t == 1, hi, zero)))
    return jnp.concatenate(out, axis=0)

def eval_kernel(cid, fid, cdim, clev, fdim, flev, tfp, tw, G, Fo, Fx, states, shock, g_ref, sav, prices, T, J, cap, ST):
    step = pl.program_id(0)
    @pl.when(step == 0)
    def _():
        J[...] = lax.broadcasted_iota(jnp.int32, (128, 128), 0).astype(jnp.float32).astype(jnp.bfloat16)
        own = g_ref[0]
        for k in range(32):
            o = Fo[:, :, pl.ds(128 * k, 128)].reshape(120, 128)
            f = Fx[:, :, pl.ds(128 * k, 128)].reshape(120, 128)
            T[own, k, pl.ds(0, 120), :] = o
            T[1 - own, k, pl.ds(0, 120), :] = f
    for i in range(TPS):
        ST[pl.ds(64 * i, 59), :] = states[:, pl.ds(128 * i, 128)]
    def tile(i, _):
        t = step * TPS + i
        lane0 = pl.multiple_of(i * 128, 128)
        phis, left = [], [[], []]
        for k in range(8):
            b = cid[t * 8 + k]
            phis.append(hat_rows(ST, i, cdim[b], clev[b], J))
            at = ((b % 2) * 8 + (b // 2) % 4) * 16 + (b // 32) * 4 + (b // 8) % 4
            left[0].append(G[at, pl.ds(0, 120), :])
            left[1].append(G[at + 64, pl.ds(0, 120), :])
        for k in range(8):
            b = fid[t * 8 + k]
            phis.append(hat_rows(ST, i, fdim[b], flev[b], J))
            left[0].append(T[0, b, pl.ds(0, 120), :])
            left[1].append(T[1, b, pl.ds(0, 120), :])
        phi = jnp.concatenate(phis, axis=0)
        total = jnp.zeros((8, 128), jnp.float32)
        for h in range(2):
            acc = jnp.dot(jnp.concatenate(left[h], axis=1), phi, preferred_element_type=jnp.float32)
            s = jnp.exp(acc).astype(jnp.bfloat16)
            sav[pl.ds(30 * h, 30), :, pl.ds(lane0, 128)] = s.reshape(30, 4, 128)
            total += jnp.sum(s.astype(jnp.float32).reshape(15, 8, 128), axis=0)
        cap[:, pl.ds(lane0, 128)] = (total[:4] + total[4:])
        return 0
    lax.fori_loop(0, TPS, tile, 0)
    W = TPS * 128
    capital = cap[...] * (1.0 / 60.0)
    sub = lax.broadcasted_iota(jnp.int32, (4, W), 0)
    tf = jnp.where(sub == 0, tfp[0], jnp.where(sub == 1, tfp[1], jnp.where(sub == 2, tfp[2], tfp[3])))
    logc = jnp.log(capital)
    interest = 0.33 * tf * jnp.exp(logc * (0.33 - 1.0)) + 1.0 - 0.1
    earnings = (1.0 - 0.33) * tf * jnp.exp(logc * 0.33)
    sh = jnp.concatenate([shock[pl.ds(step * TPS + i, 1), :] for i in range(TPS)], axis=1)
    w = jnp.zeros((4, W), jnp.float32)
    for k in range(4):
        col = jnp.where(sub == 0, tw[k * 4], jnp.where(sub == 1, tw[k * 4 + 1], jnp.where(sub == 2, tw[k * 4 + 2], tw[k * 4 + 3])))
        den = tw[k * 4] + tw[k * 4 + 1] + tw[k * 4 + 2] + tw[k * 4 + 3]
        w = jnp.where(sh == k, col / den, w)
    prices[0:1, :] = jnp.sum(w * interest, axis=0, keepdims=True)
    prices[1:2, :] = jnp.sum(w * earnings, axis=0, keepdims=True)

def evaluate(cid, fid, cdim, clev, fdim, flev, tfp, tw, G, Fo, Fx, states, shock, g):
    n = states.shape[1]
    steps = n // (TPS * 128)
    smem = pl.BlockSpec(memory_space=pltpu.SMEM)
    vmem = pl.BlockSpec(memory_space=pltpu.VMEM)
    sav, prices = pl.pallas_call(
        eval_kernel,
        grid=(steps,),
        out_shape=(jax.ShapeDtypeStruct((60, 4, n), jnp.bfloat16), jax.ShapeDtypeStruct((2, n), jnp.float32)),
        in_specs=[smem] * 8 + [vmem] * 3 + [pl.BlockSpec((59, TPS * 128), lambda i: (0, i)), vmem, smem],
        out_specs=(pl.BlockSpec((60, 4, TPS * 128), lambda i: (0, 0, i)), pl.BlockSpec((2, TPS * 128), lambda i: (0, i))),
        scratch_shapes=[pltpu.VMEM((2, 32, 128, 128), jnp.bfloat16), pltpu.VMEM((128, 128), jnp.bfloat16), pltpu.VMEM((4, TPS * 128), jnp.float32), pltpu.VMEM((TPS * 64, 128), jnp.float32)],
        compiler_params=pltpu.CompilerParams(vmem_limit_bytes=60 << 20),
        name="evaluate",
    )(cid, fid, cdim, clev, fdim, flev, tfp, tw, G, Fo, Fx, states, shock, g)
    return sav, prices


def body(
    grid_states,
    coarse_active,
    fine_active,
    shock,
    coarse_surplus,
    fine_surplus,
    coarse_dim,
    coarse_level,
    fine_dim,
    fine_level,
    tfp,
    trans_weight,
):
    coarse = coarse_surplus.transpose(1, 0, 2).reshape(120, 128)
    rows = lax.broadcasted_iota(jnp.int32, (8, 128), 0)
    described = jnp.where(rows == 0, coarse_dim[0], coarse_level[0]).astype(jnp.bfloat16)
    piece = jnp.concatenate([coarse, described], axis=0)
    fine = fine_surplus.transpose(1, 0, 2)
    gathered, other = gather(piece, fine)
    told = gathered[:, :4, :, :, 120:122, 0].transpose(2, 3, 1, 0, 4).reshape(128, 2).astype(jnp.int32)
    savings, prices = evaluate(
        coarse_active.reshape(-1),
        fine_active.reshape(-1),
        told[:, 0],
        told[:, 1],
        fine_dim,
        fine_level,
        tfp,
        trans_weight.reshape(-1),
        gathered.reshape(256, 128, 128),
        fine,
        other,
        grid_states,
        shock.reshape(-1, 128),
        lax.axis_index("grp").reshape(1).astype(jnp.int32),
    )
    return (savings.transpose(1, 0, 2), prices)


def solution(mesh):
    in_specs = (
        P(None, ("pts", "grp")),
        P(("pts", "grp"), None),
        P(("pts", "grp"), None),
        P(("pts", "grp")),
        P(None, "grp", "pts"),
        P(None, "grp", "pts"),
        P("pts"),
        P("pts"),
        P("pts"),
        P("pts"),
        P(),
        P(),
    )
    out_specs = (P(None, None, ("pts", "grp")), P(None, ("pts", "grp")))
    return jax.shard_map(body, mesh=mesh, in_specs=in_specs, out_specs=out_specs, check_vma=False)
```

time: 542 us -> 117 us (0.22); the launches traced: 536 us -> 117 us
  waiting for transfers between devices: 236 us -> 0 us
  local copies, waits for them, and re-layouts: 180 us -> 5.94 us
  Pallas kernels: 0 us -> 107 us
  matrix products: 52.4 us -> 0 us
  blocking collectives: 31.7 us -> 0 us
  other arithmetic: 20.9 us -> 2.48 us
  between operations: 15.4 us -> 1.95 us
    all_gather x2 -> x0, waiting for transfers between devices: 235 us -> none  [the longest x1 212 us: body(): lax.all_gather(coarse_gens, 'pts', axis=2, tiled=True)]
    gather x48 -> x0, local copies, waits for them, and re-layouts: 113 us -> none  [the longest x8 83.5 us: one_tile(): coef = table[block_ids]]
    pallas_call x0 -> x2, Pallas kernels: none -> 107 us  [the longest x1 58.5 us: gather(): pl.pallas_call(gather_kernel, out_shape=(jax.ShapeDtypeStruct((2, 8, 4, 4...]
    dot_general x9 -> x0, matrix products: 52.4 us -> none  [the longest x8 51.7 us: one_tile(): jnp.einsum('kgj,kjt->gt', coef, phi, preferred_element_type=jnp.float32)]
    unnamed x14 -> x2, local copies, waits for them, and re-layouts: 23.3 us -> 1.54 us
    unnamed x1 -> x0, blocking collectives: 20.8 us -> none
    all_gather x2 -> x0, local copies, waits for them, and re-layouts: 13.5 us -> none  [the longest x1 10.9 us: body(): lax.all_gather(coarse_gens, 'pts', axis=2, tiled=True)]
    all_gather x1 -> x0, blocking collectives: 10.8 us -> none  [body(): lax.all_gather(coarse_surplus, 'grp', axis=1, tiled=True)]
  transfers between devices with their start and end apart: 2 -> 0, of which waited for: 2 -> 0; matrix products, arithmetic and copies ran while one was open for 3% -> 0% of each run, Pallas kernels for 0% -> 0%
where the time goes in v1:
time: 117 us
  Pallas kernels  107 us (91%)
  local copies, waits for them, and re-layouts  5.94 us (5%)
  other arithmetic  2.48 us (2%)
  between operations  1.95 us (2%)
    pallas_call x1, Pallas kernels, gather(): pl.pallas_call(gather_kernel, out_shape=(jax.ShapeDtypeStruct((2, 8, 4, 4...  58.5 us
    pallas_call x1, Pallas kernels, evaluate(): pl.pallas_call(eval_kernel, grid=(steps,), out_shape=(jax.ShapeDtypeStruc...  48 us

profile of v1, /device:TPU:36, one launch (start us, length us, event | category | flops | bytes accessed | tf_op | source)
XLA Modules:
  0.0 116.9 jit_solution(1900729419319434954)
XLA Ops:
  1.9 0.1 pad.1.clone
  2.0 1.3 %reshape.33.tw = f32[16]{0:T(128)} reshape(f32[4,4]{1,0:T(4,128)} %param.23) | data formatting | bytes 128 | tf_op jit(solution)/shard_map/reshape | solution.py:196
  3.4 1.5 %pad_maximum_fusion.piece = bf16[128,128]{1,0:T(8,128)(2,1)} fusion(bf16[120,128]{1,0:T(8,128)(2,1)} %bitcast.26, bf16[128]{0:T(256)(128)(2,1)S(1)} %pad.1.clone), kind=kLoop, calls=%fused_computation.1 | loop fusion | flops 65536 | bytes 63744 | tf_op jit(solution)/shard_map/concatenate | solution.py:184
  4.8 0.8 copy.18
  5.6 0.7 reshape.30.cid
  6.3 0.8 copy.19
  7.0 0.7 reshape.31.fid
  7.7 58.5 %shard_map.131 = (bf16[2,8,4,4,128,128]{5,4,3,2,1,0:T(8,128)(2,1)}, bf16[30,4,4096]{2,1,0:T(4,128)(2,1)}) custom-call(bf16[128,128]{1,0:T(8,128)(2,1)} %pad_maximum_fusion.piece, bf16[30,4,4096]{2,1,0:T(4,128)(2,1)} %bitcast.22), custom_call_target="tpu_custom_call" | custom-call | tf_op jit(solution)/shard_map/pallas_call | solution.py:70
  66.3 1.0 slice_convert_fusion
  67.3 0.9 copy.22
  68.2 0.1 reshape.37
  68.3 0.6 slice_bitcast_fusion
  68.9 48.0 %evaluate.1 = (bf16[60,4,8192]{2,1,0:T(4,128)(2,1)}, f32[2,8192]{1,0:T(2,128)}) custom-call(s32[512]{0:T(512)} %reshape.30.cid, s32[512]{0:T(512)} %reshape.31.fid, s32[128]{0:T(128)} %get-tuple-element.11.cdim, s32[128]{0:T(128)} %get-tuple-element.10.clev, s32[32]{0:T(128)} %fdim.1, s32[32]{0:T(128)} %flev.1, f32[4]{0:T(128)} %tfp.1, f32[16]{0:T(128)} %reshape.33.tw, ...), custom_call_target="tpu_custom_call" | custom-call | tf_op jit(solution)/shard_map/evaluate/pallas_call | solution.py:154
  (1 shorter events, 0.0 us)

commit v2 on v1

v2 whole, which is shorter than its diff:
```python
import functools

import jax
import jax.numpy as jnp
from jax import lax
from jax.experimental import pallas as pl
from jax.experimental.pallas import tpu as pltpu
from jax.sharding import PartitionSpec as P

MESH = pl.DeviceIdType.MESH


def gather_kernel(piece, fine, G, F, zs, zr, xs, xr, ys, yr, ss, sr, fs, fr, ls):
    p, g = lax.axis_index("pts"), lax.axis_index("grp")
    c, zl, x, y = p % 2, (p // 2) % 4, (p // 8) % 4, p // 32
    z = g * 4 + zl
    def dev(x, y, z, c):
        return {"pts": ((y * 4 + x) * 4 + z % 4) * 2 + c, "grp": z // 4}
    zd = lambda d: dev(x, y, (z + d + 8) % 8, c)
    xd = lambda d: dev((x + d + 4) % 4, y, z, c)
    yd = lambda d: dev(x, (y + d + 4) % 4, z, c)
    sib = dev(x, y, z, 1 - c)
    zo, xo = (4, 3, -3, 2, -2, 1, -1), (2, 1, -1)
    b = pltpu.get_barrier_semaphore()
    partners = [zd(d) for d in zo] + [xd(d) for d in xo] + [yd(d) for d in xo] + [sib]
    for d in partners:
        pl.semaphore_signal(b, 1, device_id=d, device_id_type=MESH)
    pl.semaphore_wait(b, len(partners))
    pend = []
    def rc(src, dst, s, r, d):
        cp = pltpu.make_async_remote_copy(src, dst, s, r, device_id=d, device_id_type=MESH)
        cp.start()
        pend.append(cp)
        return cp
    own = pltpu.make_async_copy(piece, G.at[g, y, x, zl, c], ls)
    zc = [rc(piece, G.at[g, y, x, zl, c], zs.at[i], zr.at[i], zd(d)) for i, d in enumerate(zo)]
    own.start()
    rc(fine, F, fs, fr, zd(4))
    own.wait()
    for cp in zc: cp.wait_recv()
    a = G.at[0, y, x, :, c]
    bb = G.at[1, y, x, :, c]
    s1 = []
    for i, d in enumerate(xo):
        s1.append(rc(a, a, xs.at[i], xr.at[i], xd(d)))
        s1.append(rc(bb, bb, ys.at[i], yr.at[i], yd(d)))
    for cp in s1: cp.wait_recv()
    def A(yy, z0=0, nz=4): return G.at[0, yy, :, pl.ds(z0, nz), c]
    def B(xx, z0=0, nz=4): return G.at[1, :, xx, pl.ds(z0, nz), c]
    def sibs(i, ref): rc(ref, ref, ss.at[i], sr.at[i], sib)
    ym, yp, xm, xp = (y + 3) % 4, (y + 1) % 4, (x + 3) % 4, (x + 1) % 4
    y2, x2 = (y + 2) % 4, (x + 2) % 4
    u = [rc(A(y), A(y), ys.at[3], yr.at[3], yd(1)), rc(B(x), B(x), xs.at[3], xr.at[3], xd(1)),
         rc(A(y), A(y), ys.at[4], yr.at[4], yd(-1)), rc(B(x), B(x), xs.at[4], xr.at[4], xd(-1))]
    sibs(0, A(y)); sibs(1, B(x))
    v = []
    u[0].wait_recv(); v.append(rc(A(ym, 0, 2), A(ym, 0, 2), ys.at[5], yr.at[5], yd(1))); sibs(2, A(ym))
    u[1].wait_recv(); v.append(rc(B(xm, 0, 2), B(xm, 0, 2), xs.at[5], xr.at[5], xd(1))); sibs(3, B(xm))
    u[2].wait_recv(); v.append(rc(A(yp, 2, 2), A(yp, 2, 2), ys.at[6], yr.at[6], yd(-1))); sibs(4, A(yp))
    u[3].wait_recv(); v.append(rc(B(xp, 2, 2), B(xp, 2, 2), xs.at[6], xr.at[6], xd(-1))); sibs(5, B(xp))
    for cp in v: cp.wait_recv()
    sibs(6, A(y2)); sibs(7, B(x2))
    done = set(id(q) for q in zc + s1 + u + v)
    for cp in pend:
        cp.wait_send()
        if id(cp) not in done: cp.wait_recv()

def gather(piece, fine):
    dma = pltpu.SemaphoreType.DMA
    return pl.pallas_call(gather_kernel,
        out_shape=(jax.ShapeDtypeStruct((2, 4, 4, 4, 2, 128, 128), jnp.bfloat16), jax.ShapeDtypeStruct((30,4,4096), jnp.bfloat16)),
        in_specs=[pl.BlockSpec(memory_space=pl.ANY)]*2, out_specs=[pl.BlockSpec(memory_space=pl.ANY)]*2,
        scratch_shapes=[dma((7,)), dma((7,)), dma((7,)), dma((7,)), dma((7,)), dma((7,)), dma((8,)), dma((8,)), dma, dma, dma],
        compiler_params=pltpu.CompilerParams(collective_id=0, has_side_effects=True))(piece, fine)


def ACC(m):
    return pltpu.ACC(m)((128, 256), jnp.float32)

TPS = 8

def hat_rows(states, lane0, dim, level, low_ref):
    row = jnp.broadcast_to(states[pl.ds(lane0 * 64 + dim, 1), :], (8, 128))
    scale = jnp.where(level == 0, 127.0, jnp.where(level == 1, 63.5, 31.75))
    scaled = row * scale
    lower = jnp.minimum(jnp.floor(scaled), 126.0)
    part = scaled - lower
    twice = lambda v: jnp.concatenate([v, v], axis=0).astype(jnp.bfloat16)
    lo = twice(1.0 - part)
    hi = twice(1.0 - jnp.abs(part - 1.0))
    at, nx = twice(lower), twice(lower + 1.0)
    out = []
    zero = jnp.zeros((16, 128), jnp.bfloat16)
    for q in range(8):
        j = low_ref[pl.ds(16 * q, 16), :]
        out.append(jnp.where(j == at, lo, jnp.where(j == nx, hi, zero)))
    return jnp.concatenate(out, axis=0)

def eval_kernel(cid, fid, fdim, flev, tfp, tw, G, Fo, Fx, states, shock, g_ref, sav, prices, T, J, cap, ST, told_v, told, told_sem):
    step = pl.program_id(0)
    @pl.when(step == 0)
    def _():
        J[...] = lax.broadcasted_iota(jnp.int32, (128, 128), 0).astype(jnp.float32).astype(jnp.bfloat16)
        lane = lax.broadcasted_iota(jnp.int32, (8, 128), 1)
        said = jnp.zeros((8, 128), jnp.float32)
        for b in range(128):
            said = jnp.where(lane == b, G[b, pl.ds(120, 8), :].astype(jnp.float32), said)
        told_v[...] = said.astype(jnp.int32)
        telling = pltpu.make_async_copy(told_v, told, told_sem)
        telling.start()
        own = g_ref[0]
        for k in range(32):
            o = Fo[:, :, pl.ds(128 * k, 128)].reshape(120, 128)
            f = Fx[:, :, pl.ds(128 * k, 128)].reshape(120, 128)
            T[own, k, pl.ds(0, 120), :] = o
            T[1 - own, k, pl.ds(0, 120), :] = f
        telling.wait()
    for i in range(TPS):
        ST[pl.ds(64 * i, 59), :] = states[:, pl.ds(128 * i, 128)]
    def tile(accs, ii, _):
        i = ii * 2
        t = step * TPS + i
        lane0 = i * 128
        def pair(t, i, q):
            phis, left = [], [[], []]
            for k in (2 * q, 2 * q + 1):
                if k < 8:
                    b = cid[k, t]
                    phis.append(hat_rows(ST, i, told[0, b], told[1, b], J))
                    left[0].append(G[b])
                    left[1].append(G[b + 128])
                else:
                    b = fid[k - 8, t]
                    phis.append(hat_rows(ST, i, fdim[b], flev[b], J))
                    left[0].append(T[0, b])
                    left[1].append(T[1, b])
            return jnp.concatenate(phis, axis=0), [jnp.concatenate(l, axis=1) for l in left]
        for q in range(8):
            for m in range(2):
                phi, left = pair(t + m, i + m, q)
                pltpu.matmul_push_rhs(jnp.concatenate([phi, phi], axis=1), q % 2, m)
                for h in range(2):
                    pltpu.matmul_acc_lhs(accs[m][h], left[h], load_staged_rhs=q % 2 if h == 0 else None)
        for m in range(2):
            lane = lane0 + m * 128
            total = jnp.zeros((8, 128), jnp.float32)
            for h in range(2):
                a = pltpu.matmul_pop(accs[m][h])[:120, :128]
                s = jnp.exp(a).astype(jnp.bfloat16)
                sav[pl.ds(30 * h, 30), :, pl.ds(lane, 128)] = s.reshape(30, 4, 128)
                total += jnp.sum(s.astype(jnp.float32).reshape(15, 8, 128), axis=0)
            cap[:, pl.ds(lane, 128)] = (total[:4] + total[4:])
        return 0
    def scoped(*a):
        for ii in range(TPS // 2):
            o = 4 * (ii % 2)
            tile([[a[o], a[o + 1]], [a[o + 2], a[o + 3]]], ii, 0)
    pl.run_scoped(scoped, *([ACC(0), ACC(0), ACC(1), ACC(1)] * 2))
    W = TPS * 128
    capital = cap[...] * (1.0 / 60.0)
    sub = lax.broadcasted_iota(jnp.int32, (4, W), 0)
    tf = jnp.where(sub == 0, tfp[0], jnp.where(sub == 1, tfp[1], jnp.where(sub == 2, tfp[2], tfp[3])))
    logc = jnp.log(capital)
    interest = 0.33 * tf * jnp.exp(logc * (0.33 - 1.0)) + 1.0 - 0.1
    earnings = (1.0 - 0.33) * tf * jnp.exp(logc * 0.33)
    sh = jnp.concatenate([shock[pl.ds(step * TPS + i, 1), :] for i in range(TPS)], axis=1)
    w = jnp.zeros((4, W), jnp.float32)
    for k in range(4):
        col = jnp.where(sub == 0, tw[k, 0], jnp.where(sub == 1, tw[k, 1], jnp.where(sub == 2, tw[k, 2], tw[k, 3])))
        den = tw[k, 0] + tw[k, 1] + tw[k, 2] + tw[k, 3]
        w = jnp.where(sh == k, col / den, w)
    prices[0:1, :] = jnp.sum(w * interest, axis=0, keepdims=True)
    prices[1:2, :] = jnp.sum(w * earnings, axis=0, keepdims=True)

def evaluate(cid, fid, fdim, flev, tfp, tw, G, Fo, Fx, states, shock, g):
    n = states.shape[1]
    steps = n // (TPS * 128)
    smem = pl.BlockSpec(memory_space=pltpu.SMEM)
    vmem = pl.BlockSpec(memory_space=pltpu.VMEM)
    sav, prices = pl.pallas_call(
        eval_kernel,
        grid=(steps,),
        out_shape=(jax.ShapeDtypeStruct((60, 4, n), jnp.bfloat16), jax.ShapeDtypeStruct((2, n), jnp.float32)),
        in_specs=[smem] * 6 + [vmem] * 3 + [pl.BlockSpec((59, TPS * 128), lambda i: (0, i)), vmem, smem],
        out_specs=(pl.BlockSpec((60, 4, TPS * 128), lambda i: (0, 0, i)), pl.BlockSpec((2, TPS * 128), lambda i: (0, i))),
        scratch_shapes=[pltpu.VMEM((2, 32, 128, 128), jnp.bfloat16), pltpu.VMEM((128, 128), jnp.bfloat16), pltpu.VMEM((4, TPS * 128), jnp.float32), pltpu.VMEM((TPS * 64, 128), jnp.float32), pltpu.VMEM((8, 128), jnp.int32), pltpu.SMEM((8, 128), jnp.int32), pltpu.SemaphoreType.DMA],
        compiler_params=pltpu.CompilerParams(vmem_limit_bytes=60 << 20),
        name="evaluate",
    )(cid, fid, fdim, flev, tfp, tw, G, Fo, Fx, states, shock, g)
    return sav, prices


def body(
    grid_states,
    coarse_active,
    fine_active,
    shock,
    coarse_surplus,
    fine_surplus,
    coarse_dim,
    coarse_level,
    fine_dim,
    fine_level,
    tfp,
    trans_weight,
):
    coarse = coarse_surplus.transpose(1, 0, 2).reshape(120, 128)
    rows = lax.broadcasted_iota(jnp.int32, (8, 128), 0)
    described = jnp.where(rows == 0, coarse_dim[0], coarse_level[0]).astype(jnp.bfloat16)
    piece = jnp.concatenate([coarse, described], axis=0)
    fine = fine_surplus.transpose(1, 0, 2)
    gathered, other = gather(piece, fine)
    savings, prices = evaluate(
        coarse_active.T,
        fine_active.T,
        fine_dim,
        fine_level,
        tfp,
        trans_weight,
        gathered.reshape(256, 128, 128),
        fine,
        other,
        grid_states,
        shock.reshape(-1, 128),
        lax.axis_index("grp").reshape(1).astype(jnp.int32),
    )
    return (savings.transpose(1, 0, 2), prices)


def solution(mesh):
    in_specs = (
        P(None, ("pts", "grp")),
        P(("pts", "grp"), None),
        P(("pts", "grp"), None),
        P(("pts", "grp")),
        P(None, "grp", "pts"),
        P(None, "grp", "pts"),
        P("pts"),
        P("pts"),
        P("pts"),
        P("pts"),
        P(),
        P(),
    )
    out_specs = (P(None, None, ("pts", "grp")), P(None, ("pts", "grp")))
    step = jax.shard_map(body, mesh=mesh, in_specs=in_specs, out_specs=out_specs, check_vma=False)

    def run(*args):
        with jax.sharding.use_abstract_mesh(mesh.abstract_mesh):
            return step(*args)

    return run
```

time: 117 us -> 88.6 us (0.76)
  Pallas kernels: 107 us -> 85 us
  local copies, waits for them, and re-layouts: 5.94 us -> 0.08 us
    pallas_call x1, Pallas kernels: 48 us -> 26.4 us  [evaluate(): pl.pallas_call(eval_kernel, grid=(steps,), out_shape=(jax.ShapeDtypeStruc...]
    reshape x3 -> x0, local copies, waits for them, and re-layouts: 2.71 us -> none  [the longest x1 1.35 us: body(): trans_weight.reshape(-1)]
    unnamed x2 -> x0, local copies, waits for them, and re-layouts: 1.54 us -> none
where the time goes in v2:
time: 88.6 us; the launch traced here: 88.5 us
  Pallas kernels  85 us (96%)
  between operations  1.94 us (2%)
  other arithmetic  1.46 us (2%)
    pallas_call x1, Pallas kernels, gather(): pl.pallas_call(gather_kernel, out_shape=(jax.ShapeDtypeStruct((2, 4, 4, 4...  58.5 us
    pallas_call x1, Pallas kernels, evaluate(): pl.pallas_call(eval_kernel, grid=(steps,), out_shape=(jax.ShapeDtypeStruc...  26.4 us

profile of v2, /device:TPU:36, one launch (start us, length us, event | category | flops | bytes accessed | tf_op | source)
XLA Modules:
  0.0 88.5 jit_solution(12669592700981759025)
XLA Ops:
  1.9 0.1 pad.1.clone
  2.0 1.5 %pad_maximum_fusion.piece = bf16[128,128]{1,0:T(8,128)(2,1)} fusion(bf16[120,128]{1,0:T(8,128)(2,1)} %bitcast.18, bf16[128]{0:T(256)(128)(2,1)S(1)} %pad.1.clone), kind=kLoop, calls=%fused_computation | loop fusion | flops 65536 | bytes 63744 | tf_op jit(solution)/shard_map/concatenate | solution.py:210
  3.5 58.5 %shard_map.131 = (bf16[2,4,4,4,2,128,128]{6,5,4,3,2,1,0:T(8,128)(2,1)}, bf16[30,4,4096]{2,1,0:T(4,128)(2,1)}) custom-call(bf16[128,128]{1,0:T(8,128)(2,1)} %pad_maximum_fusion.piece, bf16[30,4,4096]{2,1,0:T(4,128)(2,1)} %bitcast.15), custom_call_target="tpu_custom_call" | custom-call | tf_op jit(solution)/shard_map/pallas_call | solution.py:70
  62.0 26.4 %evaluate.1 = (bf16[60,4,8192]{2,1,0:T(4,128)(2,1)}, f32[2,8192]{1,0:T(2,128)}) custom-call(s32[8,64]{1,0:T(8,128)} %bitcast.19, s32[8,64]{1,0:T(8,128)} %bitcast.20, s32[32]{0:T(128)} %fdim.1, s32[32]{0:T(128)} %flev.1, f32[4]{0:T(128)} %tfp.1, f32[4,4]{1,0:T(4,128)} %tw.1, bf16[256,128,128]{2,1,0:T(8,128)(2,1)} %bitcast.14, bf16[30,4,4096]{2,1,0:T(4,128)(2,1)} %bitcast.16, ...), custom_call_target="tpu_custom_call" | custom-call | tf_op jit(solution)/shard_map/evaluate/pallas_call | solution.py:180
  (1 shorter events, 0.0 us)

commit v3 on v2

--- a/solution.py
+++ b/solution.py
@@ -8,6 +8,10 @@
 from jax.sharding import PartitionSpec as P
 
 MESH = pl.DeviceIdType.MESH
+
+
+def stay(v):
+    return pltpu.with_memory_space_constraint(v, pltpu.HBM)
 
 
 def gather_kernel(piece, fine, G, F, zs, zr, xs, xr, ys, yr, ss, sr, fs, fr, ls):
@@ -69,15 +73,15 @@
     dma = pltpu.SemaphoreType.DMA
     return pl.pallas_call(gather_kernel,
         out_shape=(jax.ShapeDtypeStruct((2, 4, 4, 4, 2, 128, 128), jnp.bfloat16), jax.ShapeDtypeStruct((30,4,4096), jnp.bfloat16)),
-        in_specs=[pl.BlockSpec(memory_space=pl.ANY)]*2, out_specs=[pl.BlockSpec(memory_space=pl.ANY)]*2,
+        in_specs=[pl.BlockSpec(memory_space=pl.ANY)]*2, out_specs=[pl.BlockSpec(memory_space=pltpu.VMEM)]*2,
         scratch_shapes=[dma((7,)), dma((7,)), dma((7,)), dma((7,)), dma((7,)), dma((7,)), dma((8,)), dma((8,)), dma, dma, dma],
-        compiler_params=pltpu.CompilerParams(collective_id=0, has_side_effects=True))(piece, fine)
+        compiler_params=pltpu.CompilerParams(collective_id=0, has_side_effects=True, vmem_limit_bytes=16 << 20))(piece, stay(fine))
 
 
 def ACC(m):
-    return pltpu.ACC(m)((128, 256), jnp.float32)
-
-TPS = 8
+    return pltpu.ACC(m)((240, 256), jnp.float32)
+
+TPS = 16
 
 def hat_rows(states, lane0, dim, level, low_ref):
     row = jnp.broadcast_to(states[pl.ds(lane0 * 64 + dim, 1), :], (8, 128))
@@ -112,8 +116,8 @@
         for k in range(32):
             o = Fo[:, :, pl.ds(128 * k, 128)].reshape(120, 128)
             f = Fx[:, :, pl.ds(128 * k, 128)].reshape(120, 128)
-            T[own, k, pl.ds(0, 120), :] = o
-            T[1 - own, k, pl.ds(0, 120), :] = f
+            T[0, k, pl.ds(0, 120), :] = jnp.where(own == 0, o, f)
+            T[1, k, pl.ds(8, 120), :] = jnp.where(own == 0, f, o)
         telling.wait()
     for i in range(TPS):
         ST[pl.ds(64 * i, 59), :] = states[:, pl.ds(128 * i, 128)]
@@ -121,41 +125,39 @@
         i = ii * 2
         t = step * TPS + i
         lane0 = i * 128
+        upper = lax.broadcasted_iota(jnp.int32, (16, 128), 0) < 8
+        def rows_of(first, second):
+            mixed = jnp.where(upper, first[112:], second[:16])
+            return jnp.concatenate([first[:112], mixed, second[16:]], axis=0)
         def pair(t, i, q):
-            phis, left = [], [[], []]
+            phis, left = [], []
             for k in (2 * q, 2 * q + 1):
                 if k < 8:
                     b = cid[k, t]
                     phis.append(hat_rows(ST, i, told[0, b], told[1, b], J))
-                    left[0].append(G[b])
-                    left[1].append(G[b + 128])
+                    left.append(rows_of(G[b], G[b + 128]))
                 else:
                     b = fid[k - 8, t]
                     phis.append(hat_rows(ST, i, fdim[b], flev[b], J))
-                    left[0].append(T[0, b])
-                    left[1].append(T[1, b])
-            return jnp.concatenate(phis, axis=0), [jnp.concatenate(l, axis=1) for l in left]
+                    left.append(rows_of(T[0, b], T[1, b]))
+            return jnp.concatenate(phis, axis=0), jnp.concatenate(left, axis=1)
         for q in range(8):
             for m in range(2):
                 phi, left = pair(t + m, i + m, q)
                 pltpu.matmul_push_rhs(jnp.concatenate([phi, phi], axis=1), q % 2, m)
-                for h in range(2):
-                    pltpu.matmul_acc_lhs(accs[m][h], left[h], load_staged_rhs=q % 2 if h == 0 else None)
+                pltpu.matmul_acc_lhs(accs[m], left, load_staged_rhs=q % 2)
         for m in range(2):
             lane = lane0 + m * 128
-            total = jnp.zeros((8, 128), jnp.float32)
-            for h in range(2):
-                a = pltpu.matmul_pop(accs[m][h])[:120, :128]
-                s = jnp.exp(a).astype(jnp.bfloat16)
-                sav[pl.ds(30 * h, 30), :, pl.ds(lane, 128)] = s.reshape(30, 4, 128)
-                total += jnp.sum(s.astype(jnp.float32).reshape(15, 8, 128), axis=0)
-            cap[:, pl.ds(lane, 128)] = (total[:4] + total[4:])
+            s = jnp.exp(pltpu.matmul_pop(accs[m])[:, :128]).astype(jnp.bfloat16)
+            sav[:, :, pl.ds(lane, 128)] = s.reshape(60, 4, 128)
+            total = jnp.sum(s.astype(jnp.float32).reshape(30, 8, 128), axis=0)
+            cap[:, pl.ds(lane, 128)] = total[:4] + total[4:]
         return 0
     def scoped(*a):
         for ii in range(TPS // 2):
-            o = 4 * (ii % 2)
-            tile([[a[o], a[o + 1]], [a[o + 2], a[o + 3]]], ii, 0)
-    pl.run_scoped(scoped, *([ACC(0), ACC(0), ACC(1), ACC(1)] * 2))
+            o = 2 * (ii % 2)
+            tile([a[o], a[o + 1]], ii, 0)
+    pl.run_scoped(scoped, *([ACC(0), ACC(1)] * 2))
     W = TPS * 128
     capital = cap[...] * (1.0 / 60.0)
     sub = lax.broadcasted_iota(jnp.int32, (4, W), 0)
@@ -184,9 +186,9 @@
         in_specs=[smem] * 6 + [vmem] * 3 + [pl.BlockSpec((59, TPS * 128), lambda i: (0, i)), vmem, smem],
         out_specs=(pl.BlockSpec((60, 4, TPS * 128), lambda i: (0, 0, i)), pl.BlockSpec((2, TPS * 128), lambda i: (0, i))),
         scratch_shapes=[pltpu.VMEM((2, 32, 128, 128), jnp.bfloat16), pltpu.VMEM((128, 128), jnp.bfloat16), pltpu.VMEM((4, TPS * 128), jnp.float32), pltpu.VMEM((TPS * 64, 128), jnp.float32), pltpu.VMEM((8, 128), jnp.int32), pltpu.SMEM((8, 128), jnp.int32), pltpu.SemaphoreType.DMA],
-        compiler_params=pltpu.CompilerParams(vmem_limit_bytes=60 << 20),
+        compiler_params=pltpu.CompilerParams(vmem_limit_bytes=40 << 20),
         name="evaluate",
-    )(cid, fid, fdim, flev, tfp, tw, G, Fo, Fx, states, shock, g)
+    )(*(stay(v) for v in (cid, fid, fdim, flev, tfp, tw)), G, stay(Fo), Fx, stay(states), stay(shock), g)
     return sav, prices
 
 
@@ -207,7 +209,11 @@
     coarse = coarse_surplus.transpose(1, 0, 2).reshape(120, 128)
     rows = lax.broadcasted_iota(jnp.int32, (8, 128), 0)
     described = jnp.where(rows == 0, coarse_dim[0], coarse_level[0]).astype(jnp.bfloat16)
-    piece = jnp.concatenate([coarse, described], axis=0)
+    piece = jnp.where(
+        lax.axis_index("grp") == 0,
+        jnp.concatenate([coarse, described], axis=0),
+        jnp.concatenate([described, coarse], axis=0),
+    )
     fine = fine_surplus.transpose(1, 0, 2)
     gathered, other = gather(piece, fine)
     savings, prices = evaluate(

time: 88.6 us -> 82.6 us (0.932)
  Pallas kernels: 85 us -> 79.5 us
    pallas_call x1, Pallas kernels: 26.4 us -> 20.9 us  [evaluate(): pl.pallas_call(eval_kernel, grid=(steps,), out_shape=(jax.ShapeDtypeStruc...]
    concatenate x1 -> x0, other arithmetic: 1.45 us -> none  [body(): piece = jnp.concatenate([coarse, described], axis=0)]
where the time goes in v3:
time: 82.6 us; the launch traced here: 82.4 us
  Pallas kernels  79.5 us (96%)
  between operations  1.94 us (2%)
  other arithmetic  0.85 us (1%)
    pallas_call x1, Pallas kernels, gather(): pl.pallas_call(gather_kernel, out_shape=(jax.ShapeDtypeStruct((2, 4, 4, 4...  58.6 us
    pallas_call x1, Pallas kernels, evaluate(): pl.pallas_call(eval_kernel, grid=(steps,), out_shape=(jax.ShapeDtypeStruc...  20.9 us

profile of v3, /device:TPU:36, one launch (start us, length us, event | category | flops | bytes accessed | tf_op | source)
XLA Modules:
  0.0 82.4 jit_solution(9373751821826639222)
XLA Ops:
  1.9 0.1 iota.7
  2.0 0.8 %maximum_select_fusion.piece = bf16[128,128]{1,0:T(8,128)(2,1)S(1)} fusion(bf16[8,128]{1,0:T(8,128)(2,1)S(1)} %iota.7, bf16[120,128]{1,0:T(8,128)(2,1)} %bitcast.18, pred[]{:T(512)S(6)} %eq.10), kind=kLoop, calls=%fused_computation | loop fusion | flops 147456 | bytes 65537 | tf_op jit(solution)/shard_map/jit(_where)/select_n | solution.py:212
  2.9 58.6 %shard_map.131 = (bf16[2,4,4,4,2,128,128]{6,5,4,3,2,1,0:T(8,128)(2,1)S(1)}, bf16[30,4,4096]{2,1,0:T(4,128)(2,1)S(1)}) custom-call(bf16[128,128]{1,0:T(8,128)(2,1)S(1)} %maximum_select_fusion.piece, bf16[30,4,4096]{2,1,0:T(4,128)(2,1)} %bitcast.15), custom_call_target="tpu_custom_call" | custom-call | tf_op jit(solution)/shard_map/pallas_call | solution.py:74
  61.4 20.9 %evaluate.1 = (bf16[60,4,8192]{2,1,0:T(4,128)(2,1)}, f32[2,8192]{1,0:T(2,128)}) custom-call(s32[8,64]{1,0:T(8,128)} %bitcast.19, s32[8,64]{1,0:T(8,128)} %bitcast.20, s32[32]{0:T(128)} %fdim.1, s32[32]{0:T(128)} %flev.1, f32[4]{0:T(128)} %tfp.1, f32[4,4]{1,0:T(4,128)} %tw.1, bf16[256,128,128]{2,1,0:T(8,128)(2,1)S(1)} %bitcast.14, ...), custom_call_target="tpu_custom_call" | custom-call | tf_op jit(solution)/shard_map/evaluate/pallas_call | solution.py:182
  (1 shorter events, 0.0 us)

commit v4 on v3

--- a/solution.py
+++ b/solution.py
@@ -10,11 +10,36 @@
 MESH = pl.DeviceIdType.MESH
 
 
+def own_sums(fid, fdim, flev, fine, states, T, ST, part, quarter):
+    def repack(k, _):
+        T[k] = fine[:, :, pl.ds(pl.multiple_of(k * 128, 128), 128)].reshape(120, 128)
+        return 0
+    if quarter == 0:
+        lax.fori_loop(0, fine.shape[2] // 128, repack, 0)
+    J = basis()
+    def tile(t, _):
+        ST[pl.ds(0, 59), :] = states[:, pl.ds(pl.multiple_of(t * 128, 128), 128)]
+        phis, left = [], []
+        for k in range(8):
+            b = fid[k, t]
+            phis.append(hat_rows(ST, 0, fdim[b], flev[b], J))
+            left.append(T[b])
+        part[t] = jnp.dot(jnp.concatenate(left, axis=1), jnp.concatenate(phis, axis=0), preferred_element_type=jnp.float32)
+        return 0
+    size = part.shape[0] // 4
+    lax.fori_loop(quarter * size, (quarter + 1) * size, tile, 0)
+
+
+def basis():
+    rows = lax.broadcasted_iota(jnp.int32, (16, 128), 0)
+    return [(rows + 16 * q).astype(jnp.float32).astype(jnp.bfloat16) for q in range(8)]
+
+
 def stay(v):
     return pltpu.with_memory_space_constraint(v, pltpu.HBM)
 
 
-def gather_kernel(piece, fine, G, F, zs, zr, xs, xr, ys, yr, ss, sr, fs, fr, ls):
+def gather_kernel(fid, fdim, flev, piece, fine, states, G, F, part, zs, zr, xs, xr, ys, yr, ss, sr, fs, fr, ls, fine_v, states_v, T, ST, cs):
     p, g = lax.axis_index("pts"), lax.axis_index("grp")
     c, zl, x, y = p % 2, (p // 2) % 4, (p // 8) % 4, p // 32
     z = g * 4 + zl
@@ -40,6 +65,11 @@
     zc = [rc(piece, G.at[g, y, x, zl, c], zs.at[i], zr.at[i], zd(d)) for i, d in enumerate(zo)]
     own.start()
     rc(fine, F, fs, fr, zd(4))
+    loads = [pltpu.make_async_copy(fine, fine_v, cs.at[0]), pltpu.make_async_copy(states, states_v, cs.at[1])]
+    for cp in loads: cp.start()
+    for cp in loads: cp.wait()
+    work = functools.partial(own_sums, fid, fdim, flev, fine_v, states_v, T, ST, part)
+    work(0)
     own.wait()
     for cp in zc: cp.wait_recv()
     a = G.at[0, y, x, :, c]
@@ -48,6 +78,7 @@
     for i, d in enumerate(xo):
         s1.append(rc(a, a, xs.at[i], xr.at[i], xd(d)))
         s1.append(rc(bb, bb, ys.at[i], yr.at[i], yd(d)))
+    work(1)
     for cp in s1: cp.wait_recv()
     def A(yy, z0=0, nz=4): return G.at[0, yy, :, pl.ds(z0, nz), c]
     def B(xx, z0=0, nz=4): return G.at[1, :, xx, pl.ds(z0, nz), c]
@@ -57,11 +88,13 @@
     u = [rc(A(y), A(y), ys.at[3], yr.at[3], yd(1)), rc(B(x), B(x), xs.at[3], xr.at[3], xd(1)),
          rc(A(y), A(y), ys.at[4], yr.at[4], yd(-1)), rc(B(x), B(x), xs.at[4], xr.at[4], xd(-1))]
     sibs(0, A(y)); sibs(1, B(x))
+    work(2)
     v = []
     u[0].wait_recv(); v.append(rc(A(ym, 0, 2), A(ym, 0, 2), ys.at[5], yr.at[5], yd(1))); sibs(2, A(ym))
     u[1].wait_recv(); v.append(rc(B(xm, 0, 2), B(xm, 0, 2), xs.at[5], xr.at[5], xd(1))); sibs(3, B(xm))
     u[2].wait_recv(); v.append(rc(A(yp, 2, 2), A(yp, 2, 2), ys.at[6], yr.at[6], yd(-1))); sibs(4, A(yp))
     u[3].wait_recv(); v.append(rc(B(xp, 2, 2), B(xp, 2, 2), xs.at[6], xr.at[6], xd(-1))); sibs(5, B(xp))
+    work(3)
     for cp in v: cp.wait_recv()
     sibs(6, A(y2)); sibs(7, B(x2))
     done = set(id(q) for q in zc + s1 + u + v)
@@ -69,17 +102,27 @@
         cp.wait_send()
         if id(cp) not in done: cp.wait_recv()
 
-def gather(piece, fine):
+def gather(piece, fine, fid, fdim, flev, states):
     dma = pltpu.SemaphoreType.DMA
-    return pl.pallas_call(gather_kernel,
-        out_shape=(jax.ShapeDtypeStruct((2, 4, 4, 4, 2, 128, 128), jnp.bfloat16), jax.ShapeDtypeStruct((30,4,4096), jnp.bfloat16)),
-        in_specs=[pl.BlockSpec(memory_space=pl.ANY)]*2, out_specs=[pl.BlockSpec(memory_space=pltpu.VMEM)]*2,
-        scratch_shapes=[dma((7,)), dma((7,)), dma((7,)), dma((7,)), dma((7,)), dma((7,)), dma((8,)), dma((8,)), dma, dma, dma],
-        compiler_params=pltpu.CompilerParams(collective_id=0, has_side_effects=True, vmem_limit_bytes=16 << 20))(piece, stay(fine))
-
-
-def ACC(m):
-    return pltpu.ACC(m)((240, 256), jnp.float32)
+    tiles = states.shape[1] // 128
+    return pl.pallas_call(
+        gather_kernel,
+        out_shape=(
+            jax.ShapeDtypeStruct((2, 4, 4, 4, 2, 128, 128), jnp.bfloat16),
+            jax.ShapeDtypeStruct(fine.shape, jnp.bfloat16),
+            jax.ShapeDtypeStruct((tiles, 120, 128), jnp.float32),
+        ),
+        in_specs=[pl.BlockSpec(memory_space=pltpu.SMEM)] * 3 + [pl.BlockSpec(memory_space=pl.ANY)] * 3,
+        out_specs=[pl.BlockSpec(memory_space=pltpu.VMEM)] * 3,
+        scratch_shapes=[dma((7,)), dma((7,)), dma((7,)), dma((7,)), dma((7,)), dma((7,)), dma((8,)), dma((8,)), dma, dma, dma]
+        + [pltpu.VMEM(fine.shape, jnp.bfloat16), pltpu.VMEM(states.shape, jnp.float32), pltpu.VMEM((32, 120, 128), jnp.bfloat16), pltpu.VMEM((64, 128), jnp.float32), dma((2,))],
+        compiler_params=pltpu.CompilerParams(collective_id=0, has_side_effects=True, vmem_limit_bytes=24 << 20),
+        name="gather",
+    )(stay(fid), stay(fdim), stay(flev), piece, stay(fine), stay(states))
+
+
+def ACC(m, rows):
+    return pltpu.ACC(m)((rows, 256), jnp.float32)
 
 TPS = 16
 
@@ -96,15 +139,14 @@
     out = []
     zero = jnp.zeros((16, 128), jnp.bfloat16)
     for q in range(8):
-        j = low_ref[pl.ds(16 * q, 16), :]
+        j = low_ref[q]
         out.append(jnp.where(j == at, lo, jnp.where(j == nx, hi, zero)))
     return jnp.concatenate(out, axis=0)
 
-def eval_kernel(cid, fid, fdim, flev, tfp, tw, G, Fo, Fx, states, shock, g_ref, sav, prices, T, J, cap, ST, told_v, told, told_sem):
+def eval_kernel(cid, fid, fdim, flev, tfp, tw, G, Fx, part, states, shock, g_ref, sav, prices, T, cap, ST, FS, told_v, told, told_sem):
     step = pl.program_id(0)
     @pl.when(step == 0)
     def _():
-        J[...] = lax.broadcasted_iota(jnp.int32, (128, 128), 0).astype(jnp.float32).astype(jnp.bfloat16)
         lane = lax.broadcasted_iota(jnp.int32, (8, 128), 1)
         said = jnp.zeros((8, 128), jnp.float32)
         for b in range(128):
@@ -112,16 +154,15 @@
         told_v[...] = said.astype(jnp.int32)
         telling = pltpu.make_async_copy(told_v, told, told_sem)
         telling.start()
-        own = g_ref[0]
         for k in range(32):
-            o = Fo[:, :, pl.ds(128 * k, 128)].reshape(120, 128)
-            f = Fx[:, :, pl.ds(128 * k, 128)].reshape(120, 128)
-            T[0, k, pl.ds(0, 120), :] = jnp.where(own == 0, o, f)
-            T[1, k, pl.ds(8, 120), :] = jnp.where(own == 0, f, o)
+            T[k, pl.ds(0, 120), :] = Fx[:, :, pl.ds(128 * k, 128)].reshape(120, 128)
         telling.wait()
     for i in range(TPS):
         ST[pl.ds(64 * i, 59), :] = states[:, pl.ds(128 * i, 128)]
-    def tile(accs, ii, _):
+    J = basis()
+    mine = g_ref[0] == 0
+
+    def tile(accs, fines, ii, _):
         i = ii * 2
         t = step * TPS + i
         lane0 = i * 128
@@ -139,25 +180,35 @@
                 else:
                     b = fid[k - 8, t]
                     phis.append(hat_rows(ST, i, fdim[b], flev[b], J))
-                    left.append(rows_of(T[0, b], T[1, b]))
+                    left.append(T[b])
             return jnp.concatenate(phis, axis=0), jnp.concatenate(left, axis=1)
-        for q in range(8):
-            for m in range(2):
-                phi, left = pair(t + m, i + m, q)
-                pltpu.matmul_push_rhs(jnp.concatenate([phi, phi], axis=1), q % 2, m)
-                pltpu.matmul_acc_lhs(accs[m], left, load_staged_rhs=q % 2)
+        for q in (4, 5, 6, 7, 0, 1, 2, 3):
+            m, stage = q % 2, (q // 2) % 2
+            sums = accs if q < 4 else fines
+            phi0, left0 = pair(t, i, q)
+            phi1, left1 = pair(t + 1, i + 1, q)
+            pltpu.matmul_push_rhs(jnp.concatenate([phi0, phi1], axis=1), stage, m)
+            pltpu.matmul_acc_lhs(sums[m][0], left0, load_staged_rhs=stage)
+            pltpu.matmul_acc_lhs(sums[m][1], left1)
+            if q == 7:
+                for n in range(2):
+                    lanes = slice(128 * n, 128 * n + 128)
+                    FS[ii % 2, n] = pltpu.matmul_pop(fines[0][n])[:120, lanes] + pltpu.matmul_pop(fines[1][n])[:120, lanes]
         for m in range(2):
             lane = lane0 + m * 128
-            s = jnp.exp(pltpu.matmul_pop(accs[m])[:, :128]).astype(jnp.bfloat16)
+            lanes = slice(128 * m, 128 * m + 128)
+            here, there = part[i + m], FS[ii % 2, m]
+            fine = jnp.concatenate([jnp.where(mine, here, there), jnp.where(mine, there, here)], axis=0)
+            log = pltpu.matmul_pop(accs[0][m])[:, lanes] + pltpu.matmul_pop(accs[1][m])[:, lanes] + fine
+            s = jnp.exp(log).astype(jnp.bfloat16)
             sav[:, :, pl.ds(lane, 128)] = s.reshape(60, 4, 128)
             total = jnp.sum(s.astype(jnp.float32).reshape(30, 8, 128), axis=0)
             cap[:, pl.ds(lane, 128)] = total[:4] + total[4:]
         return 0
     def scoped(*a):
         for ii in range(TPS // 2):
-            o = 2 * (ii % 2)
-            tile([a[o], a[o + 1]], ii, 0)
-    pl.run_scoped(scoped, *([ACC(0), ACC(1)] * 2))
+            tile((a[0:2], a[2:4]), (a[4:6], a[6:8]), ii, 0)
+    pl.run_scoped(scoped, *(ACC(m, rows) for rows in (240, 128) for m in (0, 0, 1, 1)))
     W = TPS * 128
     capital = cap[...] * (1.0 / 60.0)
     sub = lax.broadcasted_iota(jnp.int32, (4, W), 0)
@@ -174,7 +225,7 @@
     prices[0:1, :] = jnp.sum(w * interest, axis=0, keepdims=True)
     prices[1:2, :] = jnp.sum(w * earnings, axis=0, keepdims=True)
 
-def evaluate(cid, fid, fdim, flev, tfp, tw, G, Fo, Fx, states, shock, g):
+def evaluate(cid, fid, fdim, flev, tfp, tw, G, Fx, part, states, shock, g):
     n = states.shape[1]
     steps = n // (TPS * 128)
     smem = pl.BlockSpec(memory_space=pltpu.SMEM)
@@ -183,12 +234,12 @@
         eval_kernel,
         grid=(steps,),
         out_shape=(jax.ShapeDtypeStruct((60, 4, n), jnp.bfloat16), jax.ShapeDtypeStruct((2, n), jnp.float32)),
-        in_specs=[smem] * 6 + [vmem] * 3 + [pl.BlockSpec((59, TPS * 128), lambda i: (0, i)), vmem, smem],
+        in_specs=[smem] * 6 + [vmem] * 2 + [pl.BlockSpec((TPS, 120, 128), lambda i: (i, 0, 0)), pl.BlockSpec((59, TPS * 128), lambda i: (0, i)), vmem, smem],
         out_specs=(pl.BlockSpec((60, 4, TPS * 128), lambda i: (0, 0, i)), pl.BlockSpec((2, TPS * 128), lambda i: (0, i))),
-        scratch_shapes=[pltpu.VMEM((2, 32, 128, 128), jnp.bfloat16), pltpu.VMEM((128, 128), jnp.bfloat16), pltpu.VMEM((4, TPS * 128), jnp.float32), pltpu.VMEM((TPS * 64, 128), jnp.float32), pltpu.VMEM((8, 128), jnp.int32), pltpu.SMEM((8, 128), jnp.int32), pltpu.SemaphoreType.DMA],
+        scratch_shapes=[pltpu.VMEM((32, 128, 128), jnp.bfloat16), pltpu.VMEM((4, TPS * 128), jnp.float32), pltpu.VMEM((TPS * 64, 128), jnp.float32), pltpu.VMEM((2, 2, 120, 128), jnp.float32), pltpu.VMEM((8, 128), jnp.int32), pltpu.SMEM((8, 128), jnp.int32), pltpu.SemaphoreType.DMA],
         compiler_params=pltpu.CompilerParams(vmem_limit_bytes=40 << 20),
         name="evaluate",
-    )(*(stay(v) for v in (cid, fid, fdim, flev, tfp, tw)), G, stay(Fo), Fx, stay(states), stay(shock), g)
+    )(*(stay(v) for v in (cid, fid, fdim, flev, tfp, tw)), G, Fx, part, stay(states), stay(shock), g)
     return sav, prices
 
 
@@ -215,7 +266,7 @@
         jnp.concatenate([described, coarse], axis=0),
     )
     fine = fine_surplus.transpose(1, 0, 2)
-    gathered, other = gather(piece, fine)
+    gathered, other, part = gather(piece, fine, fine_active.T, fine_dim, fine_level, grid_states)
     savings, prices = evaluate(
         coarse_active.T,
         fine_active.T,
@@ -224,8 +275,8 @@
         tfp,
         trans_weight,
         gathered.reshape(256, 128, 128),
-        fine,
         other,
+        part,
         grid_states,
         shock.reshape(-1, 128),
         lax.axis_index("grp").reshape(1).astype(jnp.int32),

time: 82.6 us -> 79.2 us (0.959)
  Pallas kernels: 79.5 us -> 76.1 us
    pallas_call x1, Pallas kernels: 20.9 us -> 16.7 us  [evaluate(): pl.pallas_call(eval_kernel, grid=(steps,), out_shape=(jax.ShapeDtypeStruc...]
where the time goes in v4:
time: 79.2 us; the launch traced here: 78.9 us
  Pallas kernels  76.1 us (96%)
  between operations  1.94 us (2%)
  other arithmetic  0.85 us (1%)
    pallas_call x1, Pallas kernels, gather(): pl.pallas_call(gather_kernel, out_shape=(jax.ShapeDtypeStruct((2, 4, 4, 4...  59.3 us
    pallas_call x1, Pallas kernels, evaluate(): pl.pallas_call(eval_kernel, grid=(steps,), out_shape=(jax.ShapeDtypeStruc...  16.7 us

profile of v4, /device:TPU:36, one launch (start us, length us, event | category | flops | bytes accessed | tf_op | source)
XLA Modules:
  0.0 78.9 jit_solution(9654284916313960200)
XLA Ops:
  1.9 0.1 iota.7
  2.0 0.8 %maximum_select_fusion.piece = bf16[128,128]{1,0:T(8,128)(2,1)S(1)} fusion(bf16[8,128]{1,0:T(8,128)(2,1)S(1)} %iota.7, bf16[120,128]{1,0:T(8,128)(2,1)} %bitcast.17, pred[]{:T(512)S(6)} %eq.10), kind=kLoop, calls=%fused_computation | loop fusion | flops 147456 | bytes 65537 | tf_op jit(solution)/shard_map/jit(_where)/select_n | solution.py:263
  2.9 59.3 %gather.1 = (bf16[2,4,4,4,2,128,128]{6,5,4,3,2,1,0:T(8,128)(2,1)S(1)}, bf16[30,4,4096]{2,1,0:T(4,128)(2,1)S(1)}, f32[64,120,128]{2,1,0:T(8,128)S(1)}) custom-call(s32[8,64]{1,0:T(8,128)} %bitcast.18, s32[32]{0:T(128)} %fdim.3, s32[32]{0:T(128)} %flev.3, bf16[128,128]{1,0:T(8,128)(2,1)S(1)} %maximum_select_fusion.piece, bf16[30,4,4096]{2,1,0:T(4,128)(2,1)} %bitcast.15, ...), custom_call_target="tpu_custom_call" | custom-call | tf_op jit(solution)/shard_map/gather/pallas_call | solution.py:108
  62.2 16.7 %evaluate.1 = (bf16[60,4,8192]{2,1,0:T(4,128)(2,1)}, f32[2,8192]{1,0:T(2,128)}) custom-call(s32[8,64]{1,0:T(8,128)} %bitcast.20, s32[8,64]{1,0:T(8,128)} %bitcast.19, s32[32]{0:T(128)} %fdim.3, s32[32]{0:T(128)} %flev.3, f32[4]{0:T(128)} %tfp.1, f32[4,4]{1,0:T(4,128)} %tw.1, bf16[256,128,128]{2,1,0:T(8,128)(2,1)S(1)} %bitcast.14, ...), custom_call_target="tpu_custom_call" | custom-call | tf_op jit(solution)/shard_map/evaluate/pallas_call | solution.py:233
  (1 shorter events, 0.0 us)

commit v5 on v4

--- a/solution.py
+++ b/solution.py
@@ -39,7 +39,7 @@
     return pltpu.with_memory_space_constraint(v, pltpu.HBM)
 
 
-def gather_kernel(fid, fdim, flev, piece, fine, states, G, F, part, zs, zr, xs, xr, ys, yr, ss, sr, fs, fr, ls, fine_v, states_v, T, ST, cs):
+def gather_kernel(ids, dims, levels, piece, fine, states, G, F, part, zs, zr, xs, xr, ys, yr, ss, sr, fs, fr, ls, fine_v, states_v, T, ST, fid, fdim, flev, cs):
     p, g = lax.axis_index("pts"), lax.axis_index("grp")
     c, zl, x, y = p % 2, (p // 2) % 4, (p // 8) % 4, p // 32
     z = g * 4 + zl
@@ -65,7 +65,8 @@
     zc = [rc(piece, G.at[g, y, x, zl, c], zs.at[i], zr.at[i], zd(d)) for i, d in enumerate(zo)]
     own.start()
     rc(fine, F, fs, fr, zd(4))
-    loads = [pltpu.make_async_copy(fine, fine_v, cs.at[0]), pltpu.make_async_copy(states, states_v, cs.at[1])]
+    pairs = ((fine, fine_v), (states, states_v), (ids, fid), (dims, fdim), (levels, flev))
+    loads = [pltpu.make_async_copy(a, b, cs.at[i]) for i, (a, b) in enumerate(pairs)]
     for cp in loads: cp.start()
     for cp in loads: cp.wait()
     work = functools.partial(own_sums, fid, fdim, flev, fine_v, states_v, T, ST, part)
@@ -112,10 +113,12 @@
             jax.ShapeDtypeStruct(fine.shape, jnp.bfloat16),
             jax.ShapeDtypeStruct((tiles, 120, 128), jnp.float32),
         ),
-        in_specs=[pl.BlockSpec(memory_space=pltpu.SMEM)] * 3 + [pl.BlockSpec(memory_space=pl.ANY)] * 3,
+        in_specs=[pl.BlockSpec(memory_space=pl.ANY)] * 6,
         out_specs=[pl.BlockSpec(memory_space=pltpu.VMEM)] * 3,
         scratch_shapes=[dma((7,)), dma((7,)), dma((7,)), dma((7,)), dma((7,)), dma((7,)), dma((8,)), dma((8,)), dma, dma, dma]
-        + [pltpu.VMEM(fine.shape, jnp.bfloat16), pltpu.VMEM(states.shape, jnp.float32), pltpu.VMEM((32, 120, 128), jnp.bfloat16), pltpu.VMEM((64, 128), jnp.float32), dma((2,))],
+        + [pltpu.VMEM(fine.shape, jnp.bfloat16), pltpu.VMEM(states.shape, jnp.float32), pltpu.VMEM((32, 120, 128), jnp.bfloat16), pltpu.VMEM((64, 128), jnp.float32)]
+        + [pltpu.SMEM(v.shape, jnp.int32) for v in (fid, fdim, flev)]
+        + [dma((5,))],
         compiler_params=pltpu.CompilerParams(collective_id=0, has_side_effects=True, vmem_limit_bytes=24 << 20),
         name="gather",
     )(stay(fid), stay(fdim), stay(flev), piece, stay(fine), stay(states))

time: 79.2 us -> 78.4 us (0.990)
  Pallas kernels: 76.1 us -> 75.3 us
where the time goes in v5:
time: 78.4 us; the launch traced here: 78.2 us
  Pallas kernels  75.3 us (96%)
  between operations  1.94 us (2%)
  other arithmetic  0.85 us (1%)
    pallas_call x1, Pallas kernels, gather(): pl.pallas_call(gather_kernel, out_shape=(jax.ShapeDtypeStruct((2, 4, 4, 4...  58.6 us
    pallas_call x1, Pallas kernels, evaluate(): pl.pallas_call(eval_kernel, grid=(steps,), out_shape=(jax.ShapeDtypeStruc...  16.7 us

profile of v5, /device:TPU:36, one launch (start us, length us, event | category | flops | bytes accessed | tf_op | source)
XLA Modules:
  0.0 78.2 jit_solution(4909474631821834207)
XLA Ops:
  1.9 0.1 iota.7
  2.0 0.8 %maximum_select_fusion.piece = bf16[128,128]{1,0:T(8,128)(2,1)S(1)} fusion(bf16[8,128]{1,0:T(8,128)(2,1)S(1)} %iota.7, bf16[120,128]{1,0:T(8,128)(2,1)} %bitcast.17, pred[]{:T(512)S(6)} %eq.10), kind=kLoop, calls=%fused_computation | loop fusion | flops 147456 | bytes 65537 | tf_op jit(solution)/shard_map/jit(_where)/select_n | solution.py:266
  2.9 58.6 %gather.1 = (bf16[2,4,4,4,2,128,128]{6,5,4,3,2,1,0:T(8,128)(2,1)S(1)}, bf16[30,4,4096]{2,1,0:T(4,128)(2,1)S(1)}, f32[64,120,128]{2,1,0:T(8,128)S(1)}) custom-call(s32[8,64]{1,0:T(8,128)} %bitcast.18, s32[32]{0:T(128)} %fdim.1, s32[32]{0:T(128)} %flev.1, bf16[128,128]{1,0:T(8,128)(2,1)S(1)} %maximum_select_fusion.piece, bf16[30,4,4096]{2,1,0:T(4,128)(2,1)} %bitcast.15, ...), custom_call_target="tpu_custom_call" | custom-call | tf_op jit(solution)/shard_map/gather/pallas_call | solution.py:109
  61.5 16.7 %evaluate.1 = (bf16[60,4,8192]{2,1,0:T(4,128)(2,1)}, f32[2,8192]{1,0:T(2,128)}) custom-call(s32[8,64]{1,0:T(8,128)} %bitcast.20, s32[8,64]{1,0:T(8,128)} %bitcast.19, s32[32]{0:T(128)} %fdim.1, s32[32]{0:T(128)} %flev.1, f32[4]{0:T(128)} %tfp.1, f32[4,4]{1,0:T(4,128)} %tw.1, bf16[256,128,128]{2,1,0:T(8,128)(2,1)S(1)} %bitcast.14, ...), custom_call_target="tpu_custom_call" | custom-call | tf_op jit(solution)/shard_map/evaluate/pallas_call | solution.py:236
  (1 shorter events, 0.0 us)
